TPU v7x, 256 devices: a whole 4x4x8 slice. The times are simulated.
256 devices in a mesh: lat: 32 (over z, x), lon: 2 (over core), ens: 4 (over y).
Axes of the slice: x: 4, y: 4, z: 8, core: 2. Of those that a mesh axis runs over, the one named last changes fastest.
Arguments:
- fields: bfloat16 [1024, 256, 256], P(('ens', 'lat'), 'lon'), parts along dimension 0, may hold values from -6 to 6
- lon_taps: float32 [256, 4, 9], replicated, may hold values from -2 to 2
- lat_taps: bfloat16 [256, 4, 6], P('lat'), may hold values from -2.5 to 2.5
- cycle_taps: bfloat16 [4, 8, 256], replicated, may hold values from -0.375 to 0.375
- band_start: int32 [256], P('lat'), may hold values from -4 to 254, as said below
- band_width: int32 [256], P('lat'), may hold values from 4 to 6, as said below
- mixing: bfloat16 [4, 256, 256], replicated, may hold values from -0.1875 to 0.1875
Outputs:
- layer_out: bfloat16 [1024, 256, 256], P(('ens', 'lat'), 'lon'), parts along dimension 0
There are 4 independent parts, one for each index of `ens`. A program takes and returns all parts, laid end to end along the dimension named above; an argument that names none is the same for every part. Nothing has to cross between parts.
Inputs may be any that keep to these rules, and one draw needn't show every extreme that they name: band_start[i] = i - 4 + s with s in 0 .. 3; s = 0 where i % 8 == 0 and s = 3 where i % 8 == 7. band_width[i] = 6 where i % 8 is 0 or 7.
All inputs are finite; a program needn't handle non-finite values.
Results may differ from a plain program's by a relative error of at most 0.0052.
Values may be sent and summed in bfloat16 or wider, within the bound.
A program may use at most 64 MiB of HBM per device.

v0:
```python
import jax
import jax.numpy as jnp
from jax import lax
from jax.sharding import PartitionSpec as P

HALO = 4


def extended_2(cells, sides, width, closed):
    for axis, dim in sides:
        count = lax.axis_size(axis)
        ends = count if closed else count - 1
        head = lax.slice_in_dim(cells, 0, width, axis=dim)
        tail = lax.slice_in_dim(cells, cells.shape[dim] - width, cells.shape[dim], axis=dim)
        cells = jnp.concatenate(
            [
                lax.ppermute(tail, axis, [(i, (i + 1) % count) for i in range(ends)]),
                cells,
                lax.ppermute(head, axis, [((i + 1) % count, i) for i in range(ends)]),
            ],
            axis=dim,
        )
    return cells


def toeplitz(coef, base, out_count, in_count, cycle_len):
    lead = coef.shape[:-1]
    window_len = out_count + in_count - 1
    tripled = jnp.concatenate([coef, coef, coef], axis=-1)
    begin = (base - in_count + 1) % cycle_len
    window = lax.dynamic_slice_in_dim(tripled, begin, window_len, len(lead))
    flipped = jnp.flip(window, axis=-1)
    rolled = jnp.roll(flipped, -(out_count - 1), axis=-1)
    tiled = jnp.tile(rolled, (1,) * len(lead) + (out_count,))
    cut = tiled[..., : out_count * (window_len - 1)]
    shaped = cut.reshape(lead + (out_count, window_len - 1))
    return shaped[..., :in_count]


def cycle_fold(coef, col_start, col_count, cycle_len, block_in):
    width_in = block_in.shape[1]
    circ = toeplitz(coef, col_start, col_count, width_in, cycle_len)
    return jnp.einsum("kpjm,pmc->kpjc", circ, block_in, preferred_element_type=jnp.float32)


def shards(fields, lon_taps, lat_taps, cycle_taps, band_start, band_width, mixing):
    row_count, col_count, chan_count = fields.shape
    basis_count = lon_taps.shape[1]
    reach_cells = (lon_taps.shape[2] - 1) // 2
    band_len = lat_taps.shape[2]
    polar_rows = row_count // 2
    lat_count = lax.axis_size("lat")
    lon_count = lax.axis_size("lon")
    cycle_len = lon_count * col_count
    lat_pos = lax.axis_index("lat")
    lon_pos = lax.axis_index("lon")
    ext_rows = row_count + 2 * HALO
    padded = extended_2(fields, (("lon", 1),), reach_cells, True)
    ext = extended_2(padded, (("lat", 0),), HALO, False)
    taps_padded = jnp.pad(lon_taps, ((HALO, HALO), (0, 0), (0, 0)))
    taps_here = lax.dynamic_slice_in_dim(taps_padded, lat_pos * row_count, ext_rows, 0)
    accum = jnp.zeros((basis_count, ext_rows, col_count, chan_count), jnp.float32)
    for offset in range(2 * reach_cells + 1):
        tap_now = jnp.transpose(taps_here[:, :, offset])
        accum = accum + tap_now[:, :, None, None] * ext[
            None, :, offset : offset + col_count, :
        ].astype(jnp.float32)
    filtered = accum.astype(jnp.bfloat16)
    at_top = lat_pos == 0
    at_bottom = lat_pos == lat_count - 1
    slot_start = jnp.where(at_top, 0, row_count - polar_rows).astype(jnp.int32)
    slot_rows = lax.dynamic_slice_in_dim(fields, slot_start, polar_rows, 0)
    col_start = lon_pos * col_count
    coef_start = jnp.where(at_top, 0, polar_rows).astype(jnp.int32)
    coef = lax.dynamic_slice_in_dim(cycle_taps, coef_start, polar_rows, 1)
    polar_sum = cycle_fold(
        coef, col_start, col_count, cycle_len, lax.all_gather(slot_rows, "lon", axis=1, tiled=True)
    )
    polar_z = polar_sum.astype(jnp.bfloat16)
    current = lax.dynamic_slice_in_dim(filtered, slot_start + HALO, polar_rows, 1)
    polar_here = jnp.where(at_top | at_bottom, polar_z, current)
    filtered = lax.dynamic_update_slice_in_dim(filtered, polar_here, slot_start + HALO, 1)
    base_row = lat_pos * row_count
    steps_band = jnp.arange(band_len, dtype=jnp.int32)
    target = band_start[:, None] - base_row + HALO + steps_band[None, :]
    usable = steps_band[None, :] < band_width[:, None]
    ext_ids = jnp.arange(ext_rows, dtype=jnp.int32)
    select = ((target[:, :, None] == ext_ids[None, None, :]) & usable[:, :, None]).astype(
        jnp.float32
    )
    band_matrix = jnp.einsum("lkt,lte->kle", lat_taps.astype(jnp.float32), select).astype(
        jnp.bfloat16
    )
    hidden = jnp.einsum(
        "kle,kejc->kljc", band_matrix, filtered, preferred_element_type=jnp.float32
    ).astype(jnp.bfloat16)
    mixed = jnp.einsum("kljc,kco->ljo", hidden, mixing, preferred_element_type=jnp.float32)
    return (fields.astype(jnp.float32) + mixed).astype(jnp.bfloat16)


def solution(mesh):
    in_specs = (
        P(("ens", "lat"), "lon", None),
        P(),
        P("lat", None, None),
        P(),
        P("lat"),
        P("lat"),
        P(),
    )
    out_specs = P(("ens", "lat"), "lon", None)
    return jax.shard_map(shards, mesh=mesh, in_specs=in_specs, out_specs=out_specs, check_vma=False)
```

profile of v0, /device:TPU:129, one launch (start us, length us, event | category | flops | bytes accessed | tf_op | source)
XLA Modules:
  0.0 42.9 jit_solution(14044471257622411911)
XLA Ops:
  0.0 0.0 copy-start
  0.0 0.8 %fusion.30 = (bf16[8,4,256]{2,1,0:T(4,128)(2,1)S(1)}, bf16[8,4,256]{2,1,0:T(4,128)(2,1)S(1)}) fusion(bf16[8,128,256]{2,1,0:T(8,128)(2,1)} %param.7), kind=kLoop, calls=%fused_computation.63 | loop fusion | bytes 65536 | tf_op jit(solution)/shard_map/slice | solution.py:14
  0.9 0.8 %collective-permute-start = (bf16[8,4,256]{2,1,0:T(4,128)(2,1)S(1)}, bf16[8,4,256]{2,1,0:T(4,128)(2,1)S(1)}, u32[]{:S(2)}, u32[]{:S(2)}) collective-permute-start(bf16[8,4,256]{2,1,0:T(4,128)(2,1)S(1)} %get-tuple-element.16), channel_id=1, source_target_pairs={{0,4},{4,0},{1,5},{5,1},{2,6},{6,2},{3,7},{7,3},{8,12},{12,8},{9,1... | collective-permute-start | bytes 49160 | tf_op jit(solution)/shard_map/ppermute | solution.py:17
  1.6 0.1 collective-permute-start.1
  1.7 0.7 %subtract_add_fusion = s32[8]{0:T(128)S(1)} fusion(s32[8]{0:T(128)} %param.11, s32[]{:T(128)S(6)} %mul.58), kind=kLoop, calls=%fused_computation.61 | loop fusion | flops 16 | bytes 68 | tf_op jit(solution)/shard_map/add | solution.py:85
  2.4 0.1 iota_add_fusion
  2.5 0.8 %copy.8 = bf16[8,4,6]{2,1,0:T(4,128)(2,1)S(1)} copy(bf16[8,4,6]{0,1,2:T(4,128)(2,1)} %param.9) | data formatting | bytes 768 | tf_op args[2]
  3.3 0.7 %iota_compare_fusion.1 = pred[8,6]{1,0:T(8,128)(4,1)S(1)} fusion(s32[8]{0:T(128)} %param.12), kind=kLoop, calls=%fused_computation.50 | loop fusion | flops 48 | bytes 80 | tf_op jit(solution)/shard_map/lt | solution.py:86
  4.0 0.7 %constant_dynamic-slice_fusion = bf16[4,4,256]{2,1,0:T(4,128)(2,1)S(1)} fusion(bf16[4,8,256]{2,1,0:T(8,128)(2,1)} %param.10, s32[]{:T(128)S(6)} %select_n.34), kind=kLoop, calls=%fused_computation.48 | loop fusion | bytes 16388 | tf_op jit(solution)/shard_map/dynamic_slice | solution.py:75
  4.7 0.3 fusion.9
  5.0 0.9 %fusion.20 = (f32[4,16]{1,0:T(4,128)S(1)}, f32[4,16]{1,0:T(4,128)S(1)}, f32[4,16]{1,0:T(4,128)S(1)}, f32[4,16]{1,0:T(4,128)S(1)}, f32[4,16]{1,0:T(4,128)S(1)}, /...) fusion(s32[]{:T(128)S(6)} %select_n.32, f32[256,4,9]{0,1,2:T(4,128)} %param.8, ...), kind=kLoop, calls=%fused_computation.52 | loop fusion | bytes 39204 | tf_op jit(solution)/shard_map/transpose | solution.py:64
  5.9 0.1 fusion.19
  6.0 0.2 slice.109
  6.2 0.1 slice.111
  6.3 0.0 collective-permute-done
  6.3 0.0 collective-permute-done.1
  6.4 1.2 %pad_maximum_fusion.1 = bf16[8,136,256]{2,1,0:T(8,128)(2,1)S(1)} fusion(bf16[8,4,256]{2,1,0:T(4,128)(2,1)S(1)} %collective-permute-done.1, bf16[8,128,256]{2,1,0:T(8,128)(2,1)} %param.7, bf16[8,4,256]{2,1,0:T(4,128)(2,1)S(1)} %collective-permute-done), kind=kLoop, calls=%fused_computation.25 | loop fusion | flops 1671168 | bytes 1114112 | tf_op jit(solution)/shard_map/concatenate | solution.py:15
  7.6 0.7 %fusion.29 = (bf16[4,136,256]{2,1,0:T(8,128)(2,1)}, bf16[4,136,256]{2,1,0:T(8,128)(2,1)S(1)}) fusion(bf16[8,136,256]{2,1,0:T(8,128)(2,1)S(1)} %pad_maximum_fusion.1), kind=kLoop, calls=%fused_computation.62 | loop fusion | bytes 1114112 | tf_op jit(solution)/shard_map/slice | solution.py:14
  8.3 3.1 %collective-permute-start.2 = (bf16[4,136,256]{2,1,0:T(8,128)(2,1)}, bf16[4,136,256]{2,1,0:T(8,128)(2,1)S(1)}, u32[]{:S(2)}, u32[]{:S(2)}) collective-permute-start(bf16[4,136,256]{2,1,0:T(8,128)(2,1)} %get-tuple-element.14), channel_id=1, source_target_pairs={{0,8},{8,16},{16,24},{24,32},{32,40},{40,48},{48,56},{56,64},{64,7... | collective-permute-start | bytes 835592 | tf_op jit(solution)/shard_map/ppermute | solution.py:17
  11.4 5.5 %collective-permute-start.3 = (bf16[4,136,256]{2,1,0:T(8,128)(2,1)S(1)}, bf16[4,136,256]{2,1,0:T(8,128)(2,1)S(1)}, u32[]{:S(2)}, u32[]{:S(2)}) collective-permute-start(bf16[4,136,256]{2,1,0:T(8,128)(2,1)S(1)} %get-tuple-element.15), channel_id=1, source_target_pairs={{8,0},{16,8},{24,16},{32,24},{40,32},{48,40},{56,48},{64,56},{72,6... | collective-permute-start | bytes 835592 | tf_op jit(solution)/shard_map/ppermute | solution.py:19
  16.9 0.1 tile.4
  17.1 4.0 %tile.10 = bf16[4,4,49024]{2,1,0:T(4,128)(2,1)} reshape(bf16[4,4,128,383]{3,2,1,0:T(8,128)(2,1)S(1)} %tile.4) | data formatting | bytes 3137536 | tf_op jit(solution)/shard_map/tile | solution.py:34
  21.1 0.0 slice-start
  21.1 1.4 %slice-done = bf16[4,4,48896]{2,1,0:T(4,128)(2,1)S(1)} async-done(((bf16[4,4,49024]{2,1,0:T(4,128)(2,1)}), bf16[4,4,48896]{2,1,0:T(4,128)(2,1)S(1)}, s32[]{:S(2)}) %slice-start) | async-done | bytes 1564696 | tf_op jit(solution)/shard_map/slice | solution.py:35
  22.5 0.0 copy-start.1
  22.5 4.4 %reshape.78 = bf16[4,4,128,382]{3,2,1,0:T(8,128)(2,1)} reshape(bf16[4,4,48896]{2,1,0:T(4,128)(2,1)S(1)} %slice-done) | data formatting | bytes 3129344 | tf_op jit(solution)/shard_map/reshape | solution.py:36
  26.9 0.1 copy.9
  27.0 0.0 copy-done.1
  27.1 2.8 %all_gather.3 = bf16[4,256,256]{2,1,0:T(8,128)(2,1)S(1)} all-gather(bf16[4,128,256]{2,1,0:T(8,128)(2,1)S(1)} %constant_dynamic-slice_fusion.1), channel_id=1, replica_groups=mesh['lat'=32,'lon'=2,'ens'=4] {'lon'}, dimensions={1}, use_global_device_ids=true | all-gather | bytes 786432 | tf_op jit(solution)/shard_map/all_gather | solution.py:77
  29.8 0.0 collective-permute-done.2
  29.9 0.0 collective-permute-done.3
  29.9 0.2 pad_maximum_fusion
  30.0 2.3 %slice_convert_fusion.8 = (f32[16,128,256]{2,1,0:T(8,128)S(1)}, f32[16,128,256]{2,1,0:T(8,128)S(1)}, f32[16,128,256]{2,1,0:T(8,128)S(1)}, f32[16,128,256]{2,1,0:...) fusion(bf16[16,136,256]{2,1,0:T(8,128)(2,1)S(1)} %pad_maximum_f, ...), kind=kLoop, calls=%fused_computation.24 | loop fusion | flops 4718592 | bytes 28311552 | tf_op jit(solution)/shard_map/convert_element_type | solution.py:67
  32.3 0.0 copy-start.2
  32.3 6.0 %add_convert_fusion = bf16[4,16,128,256]{3,2,1,0:T(8,128)(2,1)S(1)} fusion(f32[16,128,256]{2,1,0:T(8,128)S(1)} %get-tuple-element.6, f32[4,16]{1,0:T(4,128)S(1)} %get-tuple-element.26, f32[16,128,256]{2,1,0:T(8,128)S(1)} %get-tuple-element.7, f32[4,16]{1,0:T(4,128)S(1)} %get-tuple-element.19, f32[16,128,256]{2,1,0:T(8,128)S(1)} %get-tuple-element.8, ...), kind=kLoop, calls=%fused_computation | loop fusion | flops 37748736 | bytes 23070976 | tf_op jit(solution)/shard_map/convert_element_type | solution.py:68
  38.4 0.0 copy-done.2
  38.4 0.5 %fusion.6 = bf16[4,16,128,256]{3,2,1,0:T(8,128)(2,1)S(1)} fusion(bf16[4,16,128,256]{3,2,1,0:T(8,128)(2,1)S(1)} %add_convert_fusion, s32[]{:T(128)S(6)} %select_n.37, bf16[4,4,128,382]{3,2,1,0:T(8,128)(2,1)S(1)} %copy-done.2, pred[]{:T(512)S(6)} %or.3, bf16[4,256,256]{2,1,0:T(8,128)(2,1)S(1)} %all_gather.3), kind=kOutput, calls=%fused_computation.9 | convolution fusion | flops 269484032 | bytes 3670021 | tf_op jit(solution)/shard_map/kpjm,pmc->kpjc/dot_general | solution.py:43
  38.9 2.4 %fusion = bf16[4,8,128,256]{3,1,2,0:T(8,128)(2,1)S(1)} fusion(bf16[4,8,16,1]{2,1,3,0:T(8,128)(2,1)S(1)} %copy.9, bf16[4,16,128,256]{3,2,1,0:T(8,128)(2,1)S(1)} %fusion.6), kind=kOutput, calls=%fused_computation.2 | convolution fusion | flops 33554432 | bytes 6292480 | tf_op jit(solution)/shard_map/kle,kejc->kljc/dot_general | solution.py:94
  41.3 0.0 copy-done
  41.3 1.6 %fusion.8 = bf16[8,128,256]{2,1,0:T(8,128)(2,1)} fusion(bf16[4,8,128,256]{3,1,2,0:T(8,128)(2,1)S(1)} %fusion, bf16[8,128,256]{2,1,0:T(8,128)(2,1)S(1)} %copy-done.1, bf16[4,256,256]{2,1,0:T(8,128)(2,1)S(1)} %copy-done), kind=kOutput, calls=%fused_computation.11 | convolution fusion | flops 537657344 | bytes 3670016 | tf_op jit(solution)/shard_map/kljc,kco->ljo/dot_general | solution.py:97
  (4 shorter events, 0.0 us)
Async XLA Ops:
  0.0 41.3 %copy-start = (bf16[4,256,256]{2,1,0:T(8,128)(2,1)S(1)}, bf16[4,256,256]{2,1,0:T(8,128)(2,1)}, u32[]{:S(2)}) copy-start(bf16[4,256,256]{2,1,0:T(8,128)(2,1)} %param.13) | copy-start | bytes 1572868
  0.9 5.5 %collective-permute-start = (bf16[8,4,256]{2,1,0:T(4,128)(2,1)S(1)}, bf16[8,4,256]{2,1,0:T(4,128)(2,1)S(1)}, u32[]{:S(2)}, u32[]{:S(2)}) collective-permute-start(bf16[8,4,256]{2,1,0:T(4,128)(2,1)S(1)} %get-tuple-element.16), channel_id=1, source_target_pairs={{0,4},{4,0},{1,5},{5,1},{2,6},{6,2},{3,7},{7,3},{8,12},{12,8},{9,1... | collective-permute-start | bytes 49160 | tf_op jit(solution)/shard_map/ppermute | solution.py:17
  1.6 4.7 %collective-permute-start.1 = (bf16[8,4,256]{2,1,0:T(4,128)(2,1)S(1)}, bf16[8,4,256]{2,1,0:T(4,128)(2,1)S(1)}, u32[]{:S(2)}, u32[]{:S(2)}) collective-permute-start(bf16[8,4,256]{2,1,0:T(4,128)(2,1)S(1)} %get-tuple-element.17), channel_id=1, source_target_pairs={{4,0},{0,4},{5,1},{1,5},{6,2},{2,6},{7,3},{3,7},{12,8},{8,12},{13,... | collective-permute-start | bytes 49160 | tf_op jit(solution)/shard_map/ppermute | solution.py:19
  8.3 21.6 %collective-permute-start.2 = (bf16[4,136,256]{2,1,0:T(8,128)(2,1)}, bf16[4,136,256]{2,1,0:T(8,128)(2,1)S(1)}, u32[]{:S(2)}, u32[]{:S(2)}) collective-permute-start(bf16[4,136,256]{2,1,0:T(8,128)(2,1)} %get-tuple-element.14), channel_id=1, source_target_pairs={{0,8},{8,16},{16,24},{24,32},{32,40},{40,48},{48,56},{56,64},{64,7... | collective-permute-start | bytes 835592 | tf_op jit(solution)/shard_map/ppermute | solution.py:17
  11.4 18.4 %collective-permute-start.3 = (bf16[4,136,256]{2,1,0:T(8,128)(2,1)S(1)}, bf16[4,136,256]{2,1,0:T(8,128)(2,1)S(1)}, u32[]{:S(2)}, u32[]{:S(2)}) collective-permute-start(bf16[4,136,256]{2,1,0:T(8,128)(2,1)S(1)} %get-tuple-element.15), channel_id=1, source_target_pairs={{8,0},{16,8},{24,16},{32,24},{40,32},{48,40},{56,48},{64,56},{72,6... | collective-permute-start | bytes 835592 | tf_op jit(solution)/shard_map/ppermute | solution.py:19
  21.1 1.4 %slice-start = ((bf16[4,4,49024]{2,1,0:T(4,128)(2,1)}), bf16[4,4,48896]{2,1,0:T(4,128)(2,1)S(1)}, s32[]{:S(2)}) async-start(bf16[4,4,49024]{2,1,0:T(4,128)(2,1)} %tile.10), calls=%async_computation | async-start | bytes 3129344 | tf_op jit(solution)/shard_map/slice | solution.py:35
  22.5 4.6 %copy-start.1 = (bf16[8,128,256]{2,1,0:T(8,128)(2,1)S(1)}, bf16[8,128,256]{2,1,0:T(8,128)(2,1)}, u32[]{:S(2)}) copy-start(bf16[8,128,256]{2,1,0:T(8,128)(2,1)} %param.7) | copy-start | bytes 1572868
  32.3 6.1 %copy-start.2 = (bf16[4,4,128,382]{3,2,1,0:T(8,128)(2,1)S(1)}, bf16[4,4,128,382]{3,2,1,0:T(8,128)(2,1)}, u32[]{:S(2)}) copy-start(bf16[4,4,128,382]{3,2,1,0:T(8,128)(2,1)} %reshape.78) | copy-start | bytes 4694020
where the time goes:
time: 43.2 us; the launch traced here: 42.9 us
  local copies, waits for them, and re-layouts  14.5 us (34%)
  other arithmetic  11.3 us (26%)
  starting transfers between devices  9.45 us (22%)
  matrix products  4.73 us (11%)
  blocking collectives  2.78 us (6%)
    convert_element_type x1, other arithmetic, shards(): filtered = accum.astype(jnp.bfloat16)  6.03 us
    ppermute x2, starting transfers between devices, extended_2(): lax.ppermute(head, axis, [((i + 1) % count, i) for i in range(ends)])  5.59 us
    reshape x1, local copies, waits for them, and re-layouts, toeplitz(): shaped = cut.reshape(lead + (out_count, window_len - 1))  4.44 us
    another operation x2, local copies, waits for them, and re-layouts, toeplitz(): tiled = jnp.tile(rolled, (1,) * len(lead) + (out_count,))  4.13 us
    ppermute x2, starting transfers between devices, extended_2(): lax.ppermute(tail, axis, [(i, (i + 1) % count) for i in range(ends)])  3.86 us
    all_gather x1, blocking collectives, shards(): lax.all_gather(slot_rows, 'lon', axis=1, tiled=True)  2.78 us
    dot_general x1, matrix products, shards(): jnp.einsum('kle,kejc->kljc', band_matrix, filtered, preferred_element_typ...  2.38 us
    convert_element_type x1, other arithmetic, shards(): accum = accum + tap_now[:, :, None, None] * ext[None, :, offset:offset +...  2.3 us
  transfers between devices with their start and end apart: 4, of which 0 were waited for; matrix products, arithmetic and copies ran while one was open for 31% of the time, Pallas kernels for 0%

commit v1 on v0

--- a/solution.py
+++ b/solution.py
@@ -74,7 +74,13 @@
     coef_start = jnp.where(at_top, 0, polar_rows).astype(jnp.int32)
     coef = lax.dynamic_slice_in_dim(cycle_taps, coef_start, polar_rows, 1)
     polar_sum = cycle_fold(
-        coef, col_start, col_count, cycle_len, lax.all_gather(slot_rows, "lon", axis=1, tiled=True)
+        coef,
+        col_start,
+        col_count,
+        cycle_len,
+        jnp.concatenate(
+            lax.all_to_all(jnp.stack([slot_rows] * lax.axis_size("lon")), "lon", 0, 0), axis=1
+        ),
     )
     polar_z = polar_sum.astype(jnp.bfloat16)
     current = lax.dynamic_slice_in_dim(filtered, slot_start + HALO, polar_rows, 1)

time: 43.2 us -> 88.2 us (2.04)
  local copies, waits for them, and re-layouts: 14.5 us -> 47.1 us
  other arithmetic: 11.3 us -> 19.4 us
  starting transfers between devices: 9.45 us -> 13.3 us
  blocking collectives: 2.78 us -> 0 us
  matrix products: 4.73 us -> 7.42 us
    convert_element_type x1 -> x9, local copies, waits for them, and re-layouts: 0.12 us -> 25.1 us  [shards(): accum = accum + tap_now[:, :, None, None] * ext[None, :, offset:offset +...]
    dynamic_update_slice x0 -> x1, local copies, waits for them, and re-layouts: none -> 7.91 us  [shards(): lax.dynamic_update_slice_in_dim(filtered, polar_here, slot_start + HALO, 1)]
    convert_element_type x1, other arithmetic: 6.03 us -> 11.1 us  [shards(): filtered = accum.astype(jnp.bfloat16)]
    all_to_all x0 -> x1, starting transfers between devices: none -> 3.89 us  [shards(): lax.all_to_all(jnp.stack([slot_rows] * lax.axis_size('lon')), 'lon', 0, 0)]
    convert_element_type x1, other arithmetic: 2.3 us -> 5.92 us  [shards(): accum = accum + tap_now[:, :, None, None] * ext[None, :, offset:offset +...]
    all_gather x1 -> x0, blocking collectives: 2.78 us -> none  [shards(): lax.all_gather(slot_rows, 'lon', axis=1, tiled=True)]
    dot_general x1, matrix products: 0.5 us -> 2.79 us  [cycle_fold(): jnp.einsum('kpjm,pmc->kpjc', circ, block_in, preferred_element_type=jnp.f...]
    another operation x0 -> x1, local copies, waits for them, and re-layouts: none -> 0.97 us  [shards(): jnp.stack([slot_rows] * lax.axis_size('lon'))]
  transfers between devices with their start and end apart: 4 -> 5, of which waited for: 0 -> 0; matrix products, arithmetic and copies ran while one was open for 31% -> 15% of each run, Pallas kernels for 0% -> 0%
where the time goes in v1:
time: 88.2 us; the launch traced here: 87.5 us
  local copies, waits for them, and re-layouts  47.1 us (53%)
  other arithmetic  19.4 us (22%)
  starting transfers between devices  13.3 us (15%)
  matrix products  7.42 us (8%)
    convert_element_type x9, local copies, waits for them, and re-layouts, shards(): accum = accum + tap_now[:, :, None, None] * ext[None, :, offset:offset +...  25.1 us
    convert_element_type x1, other arithmetic, shards(): filtered = accum.astype(jnp.bfloat16)  11.1 us
    dynamic_update_slice x1, local copies, waits for them, and re-layouts, shards(): lax.dynamic_update_slice_in_dim(filtered, polar_here, slot_start + HALO, 1)  7.91 us
    convert_element_type x1, other arithmetic, shards(): accum = accum + tap_now[:, :, None, None] * ext[None, :, offset:offset +...  5.92 us
    ppermute x2, starting transfers between devices, extended_2(): lax.ppermute(head, axis, [((i + 1) % count, i) for i in range(ends)])  5.58 us
    reshape x1, local copies, waits for them, and re-layouts, toeplitz(): shaped = cut.reshape(lead + (out_count, window_len - 1))  4.43 us
    another operation x2, local copies, waits for them, and re-layouts, toeplitz(): tiled = jnp.tile(rolled, (1,) * len(lead) + (out_count,))  4.1 us
    all_to_all x1, starting transfers between devices, shards(): lax.all_to_all(jnp.stack([slot_rows] * lax.axis_size('lon')), 'lon', 0, 0)  3.89 us
  transfers between devices with their start and end apart: 5, of which 0 were waited for; matrix products, arithmetic and copies ran while one was open for 15% of the time, Pallas kernels for 0%

profile of v1, /device:TPU:129, one launch (start us, length us, event | category | flops | bytes accessed | tf_op | source)
XLA Modules:
  0.0 87.5 jit_solution(10823349165216634524)
XLA Ops:
  0.0 0.0 copy-start
  0.0 0.0 copy-start.1
  0.0 0.0 copy-start.6
  0.0 0.0 copy-start.7
  0.0 0.0 copy-start.8
  0.0 0.9 %fusion.34 = (bf16[8,4,256]{2,1,0:T(4,128)(2,1)S(1)}, bf16[8,4,256]{2,1,0:T(4,128)(2,1)S(1)}) fusion(bf16[8,128,256]{2,1,0:T(8,128)(2,1)} %param.7), kind=kLoop, calls=%fused_computation.62 | loop fusion | bytes 65536 | tf_op jit(solution)/shard_map/slice | solution.py:14
  0.9 0.8 collective-permute-start
  1.7 0.1 collective-permute-start.1
  1.8 1.0 %dynamic-slice_bitcast_fusion = bf16[1,4,128,256]{3,2,1,0:T(8,128)(2,1)S(1)} fusion(bf16[8,128,256]{2,1,0:T(8,128)(2,1)} %param.7, s32[]{:T(128)S(6)} %select_n.34), kind=kLoop, calls=%fused_computation.27 | loop fusion | bytes 524292 | tf_op jit(solution)/shard_map/stack | solution.py:82
  2.7 0.8 pad_maximum_fusion.2
  3.6 3.9 %all-to-all-start = ((bf16[2,4,128,256]{3,2,1,0:T(8,128)(2,1)}), bf16[2,4,128,256]{3,2,1,0:T(8,128)(2,1)S(1)}, u32[]{:S(2)}, u32[]{:S(2)}) async-start(bf16[2,4,128,256]{3,2,1,0:T(8,128)(2,1)} %pad_maximum_fusion.2), calls=%async_computation | async-start | bytes 1048576 | tf_op jit(solution)/shard_map/all_to_all | solution.py:82
  7.5 0.0 copy-done.6
  7.5 0.0 copy-done.7
  7.5 0.1 iota_add_fusion
  7.6 0.0 copy-done.8
  7.6 0.1 iota_compare_fusion.1
  7.6 0.1 fusion.22
  7.8 0.2 slice.109
  8.0 0.1 slice.111
  8.1 0.0 collective-permute-done
  8.1 0.0 collective-permute-done.1
  8.1 0.0 copy-done.1
  8.1 0.1 pad_maximum_fusion.1
  8.3 0.9 fusion.33
  9.1 3.1 %collective-permute-start.2 = (bf16[4,136,256]{2,1,0:T(8,128)(2,1)}, bf16[4,136,256]{2,1,0:T(8,128)(2,1)S(1)}, u32[]{:S(2)}, u32[]{:S(2)}) collective-permute-start(bf16[4,136,256]{2,1,0:T(8,128)(2,1)} %get-tuple-element.14), channel_id=1, source_target_pairs={{0,8},{8,16},{16,24},{24,32},{32,40},{40,48},{48,56},{56,64},{64,7... | collective-permute-start | bytes 835592 | tf_op jit(solution)/shard_map/ppermute | solution.py:17
  12.3 5.5 %collective-permute-start.3 = (bf16[4,136,256]{2,1,0:T(8,128)(2,1)}, bf16[4,136,256]{2,1,0:T(8,128)(2,1)}, u32[]{:S(2)}, u32[]{:S(2)}) collective-permute-start(bf16[4,136,256]{2,1,0:T(8,128)(2,1)} %get-tuple-element.15), channel_id=1, source_target_pairs={{8,0},{16,8},{24,16},{32,24},{40,32},{48,40},{56,48},{64,56},{72,6... | collective-permute-start | bytes 835592 | tf_op jit(solution)/shard_map/ppermute | solution.py:19
  17.8 0.1 tile.4
  17.9 4.0 %tile.10 = bf16[4,4,49024]{2,1,0:T(4,128)(2,1)} reshape(bf16[4,4,128,383]{3,2,1,0:T(8,128)(2,1)S(1)} %tile.4) | data formatting | bytes 3137536 | tf_op jit(solution)/shard_map/tile | solution.py:34
  21.9 0.0 slice-start
  21.9 1.4 %slice-done = bf16[4,4,48896]{2,1,0:T(4,128)(2,1)S(1)} async-done(((bf16[4,4,49024]{2,1,0:T(4,128)(2,1)}), bf16[4,4,48896]{2,1,0:T(4,128)(2,1)S(1)}, s32[]{:S(2)}) %slice-start) | async-done | bytes 1564696 | tf_op jit(solution)/shard_map/slice | solution.py:35
  23.3 0.0 copy-start.5
  23.3 0.0 copy-start.4
  23.3 4.4 %reshape.86 = bf16[4,4,128,382]{3,2,1,0:T(8,128)(2,1)} reshape(bf16[4,4,48896]{2,1,0:T(4,128)(2,1)S(1)} %slice-done) | data formatting | bytes 3129344 | tf_op jit(solution)/shard_map/reshape | solution.py:36
  27.7 0.0 copy-done.5
  27.7 0.1 copy.8
  27.8 0.0 all-to-all-done
  27.8 0.8 copy.18
  28.7 0.0 copy-done.4
  28.7 0.1 fusion.24
  28.8 0.2 fusion.14
  29.0 0.0 collective-permute-done.2
  29.0 0.0 collective-permute-done.3
  29.0 1.1 %pad_maximum_fusion = bf16[16,136,256]{2,1,0:T(8,128)(2,1)S(1)} fusion(bf16[4,136,256]{2,1,0:T(8,128)(2,1)} %collective-permute-done.3, bf16[8,4,256]{2,1,0:T(4,128)(2,1)S(1)} %collective-permute-done.1, bf16[8,128,256]{2,1,0:T(8,128)(2,1)S(1)} %copy-done.1, bf16[8,4,256]{2,1,0:T(4,128)(2,1)S(1)} %collective-permute-done, ...), kind=kLoop, calls=%fused_computation.11 | loop fusion | flops 5570560 | bytes 2228224 | tf_op jit(solution)/shard_map/concatenate | solution.py:15
  30.1 5.9 %slice_convert_fusion.8 = (f32[16,128,256]{2,1,0:T(8,128)S(1)}, f32[16,128,256]{2,1,0:T(8,128)}, f32[16,128,256]{2,1,0:T(8,128)}, f32[16,128,256]{2,1,0:T(8,128)...) fusion(bf16[16,136,256]{2,1,0:T(8,128)(2,1)S(1)} %pad_maximum_f, ...), kind=kLoop, calls=%fused_computation.23 | loop fusion | flops 4718592 | bytes 28311552 | tf_op jit(solution)/shard_map/convert_element_type | solution.py:67
  36.0 2.9 %copy.10 = f32[16,128,256]{1,2,0:T(8,128)} copy(f32[16,128,256]{2,1,0:T(8,128)} %get-tuple-element.13) | data formatting | bytes 4194304 | tf_op jit(solution)/shard_map/convert_element_type | solution.py:67
  38.9 2.9 %copy.11 = f32[16,128,256]{1,2,0:T(8,128)} copy(f32[16,128,256]{2,1,0:T(8,128)} %get-tuple-element.12) | data formatting | bytes 4194304 | tf_op jit(solution)/shard_map/convert_element_type | solution.py:67
  41.9 2.9 %copy.12 = f32[16,128,256]{1,2,0:T(8,128)} copy(f32[16,128,256]{2,1,0:T(8,128)} %get-tuple-element.11) | data formatting | bytes 4194304 | tf_op jit(solution)/shard_map/convert_element_type | solution.py:67
  44.8 2.9 %copy.13 = f32[16,128,256]{1,2,0:T(8,128)} copy(f32[16,128,256]{2,1,0:T(8,128)} %get-tuple-element.10) | data formatting | bytes 4194304 | tf_op jit(solution)/shard_map/convert_element_type | solution.py:67
  47.7 2.9 %copy.14 = f32[16,128,256]{1,2,0:T(8,128)} copy(f32[16,128,256]{2,1,0:T(8,128)} %get-tuple-element.9) | data formatting | bytes 4194304 | tf_op jit(solution)/shard_map/convert_element_type | solution.py:67
  50.6 2.9 %copy.15 = f32[16,128,256]{1,2,0:T(8,128)} copy(f32[16,128,256]{2,1,0:T(8,128)} %get-tuple-element.8) | data formatting | bytes 4194304 | tf_op jit(solution)/shard_map/convert_element_type | solution.py:67
  53.5 2.9 %copy.16 = f32[16,128,256]{1,2,0:T(8,128)} copy(f32[16,128,256]{2,1,0:T(8,128)} %get-tuple-element.7) | data formatting | bytes 4194304 | tf_op jit(solution)/shard_map/convert_element_type | solution.py:67
  56.4 2.9 %copy.17 = f32[16,128,256]{1,2,0:T(8,128)} copy(f32[16,128,256]{2,1,0:T(8,128)} %get-tuple-element.6) | data formatting | bytes 4194304 | tf_op jit(solution)/shard_map/convert_element_type | solution.py:67
  59.3 1.8 %copy.9 = f32[16,128,256]{1,2,0:T(8,128)} copy(f32[16,128,256]{2,1,0:T(8,128)S(1)} %get-tuple-element.5) | data formatting | bytes 4194304 | tf_op jit(solution)/shard_map/convert_element_type | solution.py:67
  61.2 0.0 copy-start.2
  61.2 0.0 copy-start.3
  61.2 11.1 %add_convert_fusion = bf16[4,16,128,256]{2,3,1,0:T(8,128)(2,1)} fusion(f32[16,128,256]{1,2,0:T(8,128)} %copy.17, f32[4,16]{1,0:T(4,128)S(1)} %get-tuple-element.26, f32[16,128,256]{1,2,0:T(8,128)} %copy.16, f32[4,16]{1,0:T(4,128)S(1)} %get-tuple-element.19, f32[16,128,256]{1,2,0:T(8,128)} %copy.15, f32[4,16]{1,0:T(4,128)S(1)} %get-tuple-element.20, ...), kind=kLoop, calls=%fused_computation | loop fusion | flops 37748736 | bytes 23070976 | tf_op jit(solution)/shard_map/convert_element_type | solution.py:68
  72.3 0.0 copy-done.2
  72.3 0.0 copy-done.3
  72.3 2.8 %fusion.7 = bf16[4,16,128,256]{2,3,1,0:T(8,128)(2,1)} fusion(bf16[4,16,128,256]{2,3,1,0:T(8,128)(2,1)} %add_convert_fusion, s32[]{:T(128)S(6)} %select_n.37, bf16[4,256,256,1]{2,1,0,3:T(8,128)(2,1)S(1)} %bitcast.68, bf16[4,4,128,382]{3,2,1,0:T(8,128)(2,1)S(1)} %copy-done.2, pred[]{:T(512)S(6)} %or.3), kind=kOutput, calls=%fused_computation.8 | convolution fusion | flops 269484032 | bytes 3670021 | tf_op jit(solution)/shard_map/kpjm,pmc->kpjc/dot_general | solution.py:43
  75.1 7.9 %copy.21 = bf16[4,16,128,256]{3,1,2,0:T(8,128)(2,1)} copy(bf16[4,16,128,256]{2,3,1,0:T(8,128)(2,1)} %fusion.7) | data formatting | bytes 8388608 | tf_op jit(solution)/shard_map/dynamic_update_slice | solution.py:88
  83.0 2.9 %convolution_convert_fusion = bf16[4,8,128,256]{3,1,2,0:T(8,128)(2,1)S(1)} fusion(bf16[4,16,128,256]{3,1,2,0:T(8,128)(2,1)} %copy.21, bf16[4,8,16,1]{2,0,1,3:T(4,128)(2,1)S(1)} %fusion.14), kind=kOutput, calls=%fused_computation.3 | convolution fusion | flops 34603008 | bytes 6292480 | tf_op jit(solution)/shard_map/kle,kejc->kljc/dot_general | solution.py:100
  85.9 0.0 copy-done
  85.9 1.6 %fusion.11 = bf16[8,128,256]{2,1,0:T(8,128)(2,1)} fusion(bf16[4,8,128,256]{3,1,2,0:T(8,128)(2,1)S(1)} %convolution_convert_fusion, bf16[8,128,256]{2,1,0:T(8,128)(2,1)S(1)} %copy-done.1, bf16[4,256,256]{2,1,0:T(8,128)(2,1)S(1)} %copy-done), kind=kOutput, calls=%fused_computation.10 | convolution fusion | flops 537657344 | bytes 3670016 | tf_op jit(solution)/shard_map/kljc,kco->ljo/dot_general | solution.py:103
  (5 shorter events, 0.0 us)
Async XLA Ops:
  0.0 85.9 %copy-start = (bf16[4,256,256]{2,1,0:T(8,128)(2,1)S(1)}, bf16[4,256,256]{2,1,0:T(8,128)(2,1)}, u32[]{:S(2)}) copy-start(bf16[4,256,256]{2,1,0:T(8,128)(2,1)} %param.13) | copy-start | bytes 1572868
  0.0 8.1 %copy-start.1 = (bf16[8,128,256]{2,1,0:T(8,128)(2,1)S(1)}, bf16[8,128,256]{2,1,0:T(8,128)(2,1)}, u32[]{:S(2)}) copy-start(bf16[8,128,256]{2,1,0:T(8,128)(2,1)} %param.7) | copy-start | bytes 1572868
  0.0 7.5 %copy-start.6 = (bf16[4,8,256]{2,1,0:T(8,128)(2,1)S(1)}, bf16[4,8,256]{2,1,0:T(8,128)(2,1)}, u32[]{:S(2)}) copy-start(bf16[4,8,256]{2,1,0:T(8,128)(2,1)} %param.10) | copy-start | bytes 49156
  0.0 7.5 %copy-start.7 = (s32[8]{0:T(128)S(1)}, s32[8]{0:T(128)}, u32[]{:S(2)}) copy-start(s32[8]{0:T(128)} %param.11) | copy-start | bytes 100
  0.0 7.6 %copy-start.8 = (s32[8]{0:T(128)S(1)}, s32[8]{0:T(128)}, u32[]{:S(2)}) copy-start(s32[8]{0:T(128)} %param.12) | copy-start | bytes 100
  0.9 7.2 %collective-permute-start = (bf16[8,4,256]{2,1,0:T(4,128)(2,1)S(1)}, bf16[8,4,256]{2,1,0:T(4,128)(2,1)S(1)}, u32[]{:S(2)}, u32[]{:S(2)}) collective-permute-start(bf16[8,4,256]{2,1,0:T(4,128)(2,1)S(1)} %get-tuple-element.16), channel_id=1, source_target_pairs={{0,4},{4,0},{1,5},{5,1},{2,6},{6,2},{3,7},{7,3},{8,12},{12,8},{9,1... | collective-permute-start | bytes 49160 | tf_op jit(solution)/shard_map/ppermute | solution.py:17
  1.7 6.4 %collective-permute-start.1 = (bf16[8,4,256]{2,1,0:T(4,128)(2,1)S(1)}, bf16[8,4,256]{2,1,0:T(4,128)(2,1)S(1)}, u32[]{:S(2)}, u32[]{:S(2)}) collective-permute-start(bf16[8,4,256]{2,1,0:T(4,128)(2,1)S(1)} %get-tuple-element.17), channel_id=1, source_target_pairs={{4,0},{0,4},{5,1},{1,5},{6,2},{2,6},{7,3},{3,7},{12,8},{8,12},{13,... | collective-permute-start | bytes 49160 | tf_op jit(solution)/shard_map/ppermute | solution.py:19
  3.6 24.3 %all-to-all-start = ((bf16[2,4,128,256]{3,2,1,0:T(8,128)(2,1)}), bf16[2,4,128,256]{3,2,1,0:T(8,128)(2,1)S(1)}, u32[]{:S(2)}, u32[]{:S(2)}) async-start(bf16[2,4,128,256]{3,2,1,0:T(8,128)(2,1)} %pad_maximum_fusion.2), calls=%async_computation | async-start | bytes 1048576 | tf_op jit(solution)/shard_map/all_to_all | solution.py:82
  9.1 19.8 %collective-permute-start.2 = (bf16[4,136,256]{2,1,0:T(8,128)(2,1)}, bf16[4,136,256]{2,1,0:T(8,128)(2,1)S(1)}, u32[]{:S(2)}, u32[]{:S(2)}) collective-permute-start(bf16[4,136,256]{2,1,0:T(8,128)(2,1)} %get-tuple-element.14), channel_id=1, source_target_pairs={{0,8},{8,16},{16,24},{24,32},{32,40},{40,48},{48,56},{56,64},{64,7... | collective-permute-start | bytes 835592 | tf_op jit(solution)/shard_map/ppermute | solution.py:17
  12.3 16.7 %collective-permute-start.3 = (bf16[4,136,256]{2,1,0:T(8,128)(2,1)}, bf16[4,136,256]{2,1,0:T(8,128)(2,1)}, u32[]{:S(2)}, u32[]{:S(2)}) collective-permute-start(bf16[4,136,256]{2,1,0:T(8,128)(2,1)} %get-tuple-element.15), channel_id=1, source_target_pairs={{8,0},{16,8},{24,16},{32,24},{40,32},{48,40},{56,48},{64,56},{72,6... | collective-permute-start | bytes 835592 | tf_op jit(solution)/shard_map/ppermute | solution.py:19
  21.9 1.4 %slice-start = ((bf16[4,4,49024]{2,1,0:T(4,128)(2,1)}), bf16[4,4,48896]{2,1,0:T(4,128)(2,1)S(1)}, s32[]{:S(2)}) async-start(bf16[4,4,49024]{2,1,0:T(4,128)(2,1)} %tile.10), calls=%async_computation.1 | async-start | bytes 3129344 | tf_op jit(solution)/shard_map/slice | solution.py:35
  23.3 4.4 %copy-start.5 = (bf16[8,4,6]{0,1,2:T(4,128)(2,1)S(1)}, bf16[8,4,6]{0,1,2:T(4,128)(2,1)}, u32[]{:S(2)}) copy-start(bf16[8,4,6]{0,1,2:T(4,128)(2,1)} %param.9) | copy-start | bytes 1156
  23.3 5.4 %copy-start.4 = (f32[256,4,9]{0,1,2:T(4,128)S(1)}, f32[256,4,9]{0,1,2:T(4,128)}, u32[]{:S(2)}) copy-start(f32[256,4,9]{0,1,2:T(4,128)} %param.8) | copy-start | bytes 110596
  61.2 11.2 %copy-start.2 = (bf16[4,4,128,382]{3,2,1,0:T(8,128)(2,1)S(1)}, bf16[4,4,128,382]{3,2,1,0:T(8,128)(2,1)}, u32[]{:S(2)}) copy-start(bf16[4,4,128,382]{3,2,1,0:T(8,128)(2,1)} %reshape.86) | copy-start | bytes 4694020
  61.2 11.2 %copy-start.3 = (bf16[2,4,128,256]{3,2,0,1:T(8,128)(2,1)S(1)}, bf16[2,4,128,256]{3,2,0,1:T(8,128)(2,1)}, u32[]{:S(2)}) copy-start(bf16[2,4,128,256]{3,2,0,1:T(8,128)(2,1)} %copy.18) | copy-start | bytes 1572868
